TPU v7x, 512 devices: a whole 4x8x8 slice. The times are simulated.
512 devices in a mesh: brick: 64 (over z, y), blk: 8 (over x, core).
Axes of the slice: x: 4, y: 8, z: 8, core: 2. Of those that a mesh axis runs over, the one named last changes fastest.
Arguments:
- parameters: float32 [4, 65536], P(None, ('brick', 'blk')), may hold values from -0.4 to 3, as said below
- sersic: float32 [65536], P(('brick', 'blk')), may hold values from 1 to 4
- psf_width: float32 [65536], P(('brick', 'blk')), may hold values from 0.8 to 2
- point_flag: int32 [65536], P(('brick', 'blk')), may hold values 0 or 1
- owner_brick: int32 [65536, 1], P(('brick', 'blk')), may hold values from 0 to 63; in each aligned block of 128 rows (0 to 127, 128 to 255, ...) at most 4 rows name the same one
- cell_index: int32 [65536], P(('brick', 'blk')), may hold values from 0 to 31
- exposure: float32 [16384, 1024], P(('brick', 'blk')), may hold values from -120 to 120
- inv_noise: float32 [16384], P(('brick', 'blk')), may hold values from 0.5 to 2
Outputs:
- updated: float32 [4, 65536], P(None, ('brick', 'blk'))
Inputs may be any that keep to these rules, and one draw needn't show every extreme that they name: `parameters`: row 0 is a flux from 0.5 to 3, rows 1 and 2 the centre's offsets within 0.4 pixels, row 3 the log radius from ln 1.5 to ln 6. `owner_brick`: the sources of one device name one brick at most 4 times.
All inputs are finite; a program needn't handle non-finite values. No bound on the sum of `point_flag` on one device may be relied on, other than what follows from the above.
Results may differ from a plain program's by a relative error of at most 0.0003.
Values sent between devices are 32-bit elements; how exact they have to be, the bound alone decides.
A program may use at most 64 MiB of HBM per device.

v0:
```python
import math
import jax
import jax.numpy as jnp
from jax import lax
from jax.sharding import PartitionSpec as P

TILE = 32
series_terms = 96
zero_point = 30.0
base_damping = 0.1
misfit_scale = 0.05
block_rows = 32
highest = lax.Precision.HIGHEST


def incomplete_gamma(shape_value, cutoff):
    term_steps = jnp.arange(1, series_terms, dtype=cutoff.dtype)
    increments = jnp.log(cutoff)[None, :] - jnp.log(shape_value[None, :] + term_steps[:, None])
    partial_logs = jnp.concatenate(
        [jnp.zeros_like(cutoff)[None, :], jnp.cumsum(increments, axis=0)], axis=0
    )
    prefactor = shape_value * jnp.log(cutoff) - cutoff - lax.lgamma(shape_value + 1.0)
    return jnp.sum(jnp.exp(prefactor[None, :] + partial_logs), axis=0)


def render(values, sersic, psf_width, point_flag):
    flux_value = values[0]
    shift_x = values[1]
    shift_y = values[2]
    log_radius = values[3]
    coords = jnp.arange(TILE, dtype=values.dtype) + 0.5 - 0.5 * TILE
    offset_y = coords[None, :] - shift_y[:, None]
    offset_x = coords[None, :] - shift_x[:, None]
    radius_sq = offset_y[:, :, None] ** 2 + offset_x[:, None, :] ** 2
    inverse_index = 1.0 / sersic
    bfactor = 2.0 * sersic - 1.0 / 3.0 + 4.0 / (405.0 * sersic)
    cutoff = bfactor * jnp.exp((math.log(0.5 * TILE) - log_radius) * inverse_index)
    log_norm = (
        jnp.log(2.0 * math.pi * sersic)
        + 2.0 * log_radius
        + lax.lgamma(2.0 * sersic)
        - 2.0 * sersic * jnp.log(bfactor)
        + jnp.log(incomplete_gamma(2.0 * sersic, cutoff))
    )
    scaled = jnp.exp(
        (0.5 * jnp.log(radius_sq) - log_radius[:, None, None]) * inverse_index[:, None, None]
    )
    galaxy = jnp.exp(-bfactor[:, None, None] * scaled - log_norm[:, None, None])
    separation = coords[:, None] - coords[None, :]
    inv_two_var = 0.5 / (psf_width * psf_width)
    norm_psf = 1.0 / (math.sqrt(2.0 * math.pi) * psf_width)
    kernel = jnp.exp(-(separation**2)[None] * inv_two_var[:, None, None]) * norm_psf[:, None, None]
    blurred = jnp.einsum("bij,bjk->bik", kernel, galaxy, precision=highest)
    blurred = jnp.einsum("bik,blk->bil", blurred, kernel, precision=highest)
    profile_y = jnp.exp(-(offset_y**2) * inv_two_var[:, None]) * norm_psf[:, None]
    profile_x = jnp.exp(-(offset_x**2) * inv_two_var[:, None]) * norm_psf[:, None]
    point_image = profile_y[:, :, None] * profile_x[:, None, :]
    shape_image = jnp.where((point_flag == 1)[:, None, None], point_image, blurred)
    return (zero_point * flux_value)[:, None] * shape_image.reshape(values.shape[1], TILE * TILE)


def source_moments(values, sersic, psf_width, point_flag, weighted_rows, weight_rows):

    def model_of(current):
        return render(current, sersic, psf_width, point_flag)

    unit_tangents = jnp.eye(4, dtype=values.dtype)[:, :, None] * jnp.ones_like(values)[None]
    jacobian = jax.vmap(lambda tangent: jax.jvp(model_of, (values,), (tangent,))[1])(unit_tangents)
    gradient = jnp.einsum("pbq,bq->pb", jacobian, weighted_rows, precision=highest)
    curvature = (
        jnp.einsum("pbq,rbq->prb", jacobian, jacobian, precision=highest)
        * weight_rows[None, None, :]
    )
    return (gradient, curvature)


def damped_solve(curvature, gradient, damping):
    system = [[curvature[first, second] for second in range(4)] for first in range(4)]
    for first in range(4):
        system[first][first] = system[first][first] + damping * (1.0 + curvature[first, first])
    factor = [[None for second in range(4)] for first in range(4)]
    for column in range(4):
        pivot = system[column][column]
        for inner in range(column):
            pivot = pivot - factor[column][inner] * factor[column][inner]
        pivot = jnp.sqrt(pivot)
        factor[column][column] = pivot
        for lower_row in range(column + 1, 4):
            entry = system[lower_row][column]
            for inner in range(column):
                entry = entry - factor[lower_row][inner] * factor[column][inner]
            factor[lower_row][column] = entry / pivot
    forward = []
    for row_at in range(4):
        entry = gradient[row_at]
        for inner in range(row_at):
            entry = entry - factor[row_at][inner] * forward[inner]
        forward.append(entry / factor[row_at][row_at])
    solution = [None, None, None, None]
    for row_at in reversed(range(4)):
        entry = forward[row_at]
        for inner in range(row_at + 1, 4):
            entry = entry - factor[inner][row_at] * solution[inner]
        solution[row_at] = entry / factor[row_at][row_at]
    return jnp.stack(solution)


def rendered_tiles(values, sersic, psf_width, point_flag):
    count = values.shape[1]
    groups = count // block_rows
    stacked = (
        values.reshape(4, groups, block_rows).transpose(1, 0, 2),
        sersic.reshape(groups, block_rows),
        psf_width.reshape(groups, block_rows),
        point_flag.reshape(groups, block_rows),
    )
    tiles = lax.map(lambda block: render(block[0], block[1], block[2], block[3]), stacked)
    return tiles.reshape(count, TILE * TILE)


def blocked_moments(values, sersic, psf_width, point_flag, weighted_rows, weight_rows):
    count = values.shape[1]
    groups = count // block_rows
    stacked = (
        values.reshape(4, groups, block_rows).transpose(1, 0, 2),
        sersic.reshape(groups, block_rows),
        psf_width.reshape(groups, block_rows),
        point_flag.reshape(groups, block_rows),
        weighted_rows.reshape(groups, block_rows, TILE * TILE),
        weight_rows.reshape(groups, block_rows),
    )
    gradient, curvature = lax.map(
        lambda block: source_moments(block[0], block[1], block[2], block[3], block[4], block[5]),
        stacked,
    )
    gradient = gradient.transpose(1, 0, 2).reshape(4, count)
    curvature = curvature.transpose(1, 2, 0, 3).reshape(4, 4, count)
    return (gradient, curvature)


def cell_residuals(exposure, weights, slot_cells, slot_tiles):
    cell_ids = jnp.arange(exposure.shape[0], dtype=jnp.int32)
    selector = (cell_ids[:, None] == slot_cells[None, :]).astype(exposure.dtype)
    model = jnp.dot(selector, slot_tiles, precision=highest)
    misfit = exposure - model
    weighted = weights[:, None] * misfit
    local_chi = jnp.sum(weighted * misfit)
    slot_rows = jnp.dot(selector.T, weighted, precision=highest)
    slot_weights = jnp.dot(selector.T, weights, precision=highest)
    return (local_chi, slot_rows, slot_weights)


def shards(parameters, sersic, psf_width, point_flag, owner_brick, cell_index, exposure, inv_noise):
    source_count = parameters.shape[1]
    bricks = lax.axis_size("brick")
    slot_count = 2 * source_count
    capacity = slot_count // bricks
    destination = owner_brick[:, 0]
    matches = (destination[:, None] == jnp.arange(bricks, dtype=jnp.int32)[None, :]).astype(
        jnp.int32
    )
    earlier = jnp.cumsum(matches, axis=0) - matches
    rank_within = jnp.sum(earlier * matches, axis=1)
    slot_of = destination * capacity + rank_within
    weights = inv_noise * inv_noise
    pixel_total = lax.axis_size("blk") * exposure.shape[0] * exposure.shape[1]
    tiles = rendered_tiles(parameters, sersic, psf_width, point_flag)
    outgoing = jnp.zeros((slot_count, tiles.shape[1]), tiles.dtype).at[slot_of].set(tiles)
    outgoing_cells = jnp.full((slot_count,), -1, jnp.int32).at[slot_of].set(cell_index)
    incoming, incoming_cells = (
        lax.all_to_all(outgoing, "brick", split_axis=0, concat_axis=0, tiled=True),
        lax.all_to_all(outgoing_cells, "brick", split_axis=0, concat_axis=0, tiled=True),
    )
    local_chi, slot_rows, slot_weights = cell_residuals(exposure, weights, incoming_cells, incoming)
    returned, returned_weights = (
        lax.all_to_all(slot_rows, "brick", split_axis=0, concat_axis=0, tiled=True),
        lax.all_to_all(slot_weights, "brick", split_axis=0, concat_axis=0, tiled=True),
    )
    gradient, curvature = blocked_moments(
        parameters, sersic, psf_width, point_flag, returned[slot_of], returned_weights[slot_of]
    )
    group_chi = lax.psum(local_chi, "blk")
    damping = base_damping + misfit_scale * group_chi / pixel_total
    return parameters + damped_solve(curvature, gradient, damping)


def solution(mesh):
    in_specs = (
        P(None, ("brick", "blk")),
        P(("brick", "blk")),
        P(("brick", "blk")),
        P(("brick", "blk")),
        P(("brick", "blk"), None),
        P(("brick", "blk")),
        P(("brick", "blk"), None),
        P(("brick", "blk")),
    )
    out_specs = P(None, ("brick", "blk"))
    return jax.shard_map(shards, mesh=mesh, in_specs=in_specs, out_specs=out_specs, check_vma=False)
```

profile of v0, /device:TPU:6, one launch (start us, length us, event | category | flops | bytes accessed | tf_op | source)
XLA Modules:
  0.0 205.0 jit_solution(13674835427051204987)
XLA Ops:
  2.4 1.1 scatter_custom_fusion
  4.2 16.6 %all-to-all-start = ((s32[64,4,1]{1,2,0:T(1,128)}), s32[64,4,1]{1,2,0:T(1,128)S(1)}, u32[]{:S(2)}, u32[]{:S(2)}) async-start(s32[64,4,1]{1,2,0:T(1,128)} %bitcast.49), calls=%async_computation | async-start | bytes 65536 | tf_op jit(solution)/shard_map/all_to_all | solution.py:172
  21.6 1.3 reshape.2269
  24.4 14.8 %while.32 = (s32[]{:T(128)}, f32[4,32,1024]{2,1,0:T(8,128)S(1)}, f32[4,4,32]{2,1,0:T(4,128)S(1)}, s32[4,32]{1,0:T(4,128)}, f32[4,32]{1,0:T(4,128)S(1)}, /*index=5*/f32[4,32]{1,0:T(4,128)S(1)}, s32[]{:T(128)}, f32[]{:T(128)}) while((s32[]{:T(128)}, f32[4,32,1024]{2,1,0:T(8,128)S(1)}, f32[4,4,32]{2,1,0:T(4,128)S(1)}, s32[4,32]{1,0:T(4,128)}, ...), condition=%wide.region_6.7_spmd, body=%wide.region_3.6_spmd.sunk | while | flops 25907552 | bytes 1019813 | solution.py:117
  25.0 1.0 fusion.172
  26.7 1.0 convolution_select_fusion.4
  28.7 1.0 fusion.172
  30.4 1.0 convolution_select_fusion.4
  32.4 1.0 fusion.172
  34.1 1.0 convolution_select_fusion.4
  36.1 1.0 fusion.172
  37.8 1.0 convolution_select_fusion.4
  39.2 1.3 scatter_custom_fusion.1
  40.5 1.3 all_to_all.32
  41.8 12.8 %all-to-all-start.1 = ((f32[64,4,1024]{2,1,0:T(4,128)}), f32[64,4,1024]{2,1,0:T(4,128)S(1)}, u32[]{:S(2)}, u32[]{:S(2)}) async-start(f32[64,4,1024]{2,1,0:T(4,128)} %all_to_all.32), calls=%async_computation.1 | async-start | bytes 2097152 | tf_op jit(solution)/shard_map/all_to_all | solution.py:171
  57.1 26.7 %all-to-all-done.1 = f32[64,4,1024]{2,1,0:T(4,128)S(1)} async-done(((f32[64,4,1024]{2,1,0:T(4,128)}), f32[64,4,1024]{2,1,0:T(4,128)S(1)}, u32[]{:S(2)}, u32[]{:S(2)}) %all-to-all-start.1) | async-done | bytes 1048608 | tf_op jit(solution)/shard_map/all_to_all | solution.py:171
  83.8 6.5 %all-to-all-start.3 = ((f32[64,4,1]{1,2,0:T(1,128)}), f32[64,4,1]{1,2,0:T(1,128)S(1)}, u32[]{:S(2)}, u32[]{:S(2)}) async-start(f32[64,4,1]{1,2,0:T(1,128)} %bitcast.55), calls=%async_computation.3 | async-start | bytes 65536 | tf_op jit(solution)/shard_map/all_to_all | solution.py:177
  90.7 1.2 fusion.107
  92.5 1.3 all_to_all.35
  93.8 8.6 %all-to-all-done.3 = f32[64,4,1]{1,2,0:T(1,128)S(1)} async-done(((f32[64,4,1]{1,2,0:T(1,128)}), f32[64,4,1]{1,2,0:T(1,128)S(1)}, u32[]{:S(2)}, u32[]{:S(2)}) %all-to-all-start.3) | async-done | bytes 1056 | tf_op jit(solution)/shard_map/all_to_all | solution.py:177
  102.3 4.7 %all-to-all-start.2 = ((f32[64,4,1024]{2,1,0:T(4,128)}), f32[64,4,1024]{2,1,0:T(4,128)S(1)}, u32[]{:S(2)}, u32[]{:S(2)}) async-start(f32[64,4,1024]{2,1,0:T(4,128)} %all_to_all.35), calls=%async_computation.2 | async-start | bytes 2097152 | tf_op jit(solution)/shard_map/all_to_all | solution.py:176
  108.3 1.3 gather_fusion.1
  109.6 11.2 %psum.7 = f32[]{:T(128)} all-reduce(f32[]{:T(128)} %get-tuple-element.534), channel_id=1, replica_groups=mesh['brick'=64,'blk'=8] {'blk'}, use_global_device_ids=true, to_apply=%region_15.16 | all-reduce | flops 1 | bytes 8 | tf_op jit(solution)/shard_map/psum | solution.py:182
  121.4 13.4 %all-to-all-done.2 = f32[64,4,1024]{2,1,0:T(4,128)S(1)} async-done(((f32[64,4,1024]{2,1,0:T(4,128)}), f32[64,4,1024]{2,1,0:T(4,128)S(1)}, u32[]{:S(2)}, u32[]{:S(2)}) %all-to-all-start.2) | async-done | bytes 1048608 | tf_op jit(solution)/shard_map/all_to_all | solution.py:176
  135.9 65.0 %while.33 = (s32[]{:T(128)}, f32[4,4,32]{2,1,0:T(4,128)}, f32[4,4,4,32]{1,2,3,0:T(4,128)S(1)}, f32[4,32,1024]{2,1,0:T(8,128)S(1)}, s32[4,32]{1,0:T(4,128)}, /*in...) while((s32[]{:T(128)}, f32[4,4,32]{2,1,0:T(4,128)}, ...), condition=%wide.region_13.14_spmd, body=%wide.region_8.13_spmd.sunk | while | flops 138444880 | bytes 6357045 | solution.py:132
  137.9 2.9 %fusion.184 = f32[32,32,4,32]{3,1,2,0:T(8,128)S(1)} fusion(f32[32,32,32]{2,1,0:T(8,128)S(1)} %get-tuple-element.723, f32[4,32]{0,1:T(8,128)S(1)} %copy.83, f32[32,32,32]{2,1,0:T(8,128)S(1)} %get-tuple-element.731, f32[32]{0:T(128)S(1)} %bitcast.320, f32[4]{0:T(128)S(1)} %get-tuple-element.732, f32[32,32,32]{2,1,0:T(8,128)S(1)} %get-tuple-element.733, ...), kind=kOutput, calls=%fused_computation.100.clone.1 | convolution fusion | flops 51576832 | bytes 955408 | tf_op jit(solution)/shard_map/while/body/eval_jaxpr/vmap(jvp(bij,bjk->bik))/dot_general | solution.py:53
  141.5 2.2 %bitcast_select_fusion.2 = f32[4,32,32,32]{3,2,0,1:T(8,128)S(1)} fusion(f32[32,32,4,32]{3,1,2,0:T(8,128)S(1)} %fusion.184, f32[4,32,32]{2,0,1:T(4,128)S(1)} %get-tuple-element.743, f32[32,32]{1,0:T(8,128)S(1)} %get-tuple-element.744, f32[32,32]{1,0:T(8,128)S(1)} %get-tuple-element.745, f32[4,32,32]{2,0,1:T(4,128)S(1)} %get-tuple-element.746, ...), kind=kOutput, calls=%fused_computation.99.clone.1 | convolution fusion | flops 50921472 | bytes 1093920 | tf_op jit(solution)/shard_map/while/body/eval_jaxpr/vmap(jvp(bik,blk->bil))/dot_general | solution.py:54
  145.8 1.1 convolution_select_fusion.5
  147.1 2.3 %fusion.187 = f32[4,4,4,32]{1,2,3,0:T(4,128)S(1)} fusion(f32[4,4,4,32]{1,2,3,0:T(4,128)S(1)} %get-tuple-element.787, s32[]{:T(128)} %get-tuple-element.785, f32[4,32,1024]{2,0,1:T(4,128)S(1)} %reshape.2358, f32[32]{0:T(128)S(1)} %get-tuple-element.747, f32[32,1024]{1,0:T(8,128)S(1)} %mul.2955, f32[4]{0:T(128)S(1)} %get-tuple-element.748, ...), kind=kOutput, calls=%fused_computation.113.clone.1 | convolution fusion | flops 6685184 | bytes 722436 | tf_op jit(solution)/shard_map/while/body/eval_jaxpr/pbq,rbq->prb/dot_general | solution.py:71
  149.4 2.2 %fusion.186 = f32[32,1,4]{2,1,0:T(1,128)S(1)} fusion(f32[4,32,1024]{2,0,1:T(4,128)S(1)} %reshape.2358, f32[32]{0:T(128)S(1)} %get-tuple-element.747, f32[32,1024]{1,0:T(8,128)S(1)} %mul.2955, f32[4]{0:T(128)S(1)} %get-tuple-element.748, f32[32,1024,1]{1,0,2:T(8,128)S(1)} %dynamic-slice_bitcast_fusion.2), kind=kOutput, calls=%fused_computation.131.clone.1 | convolution fusion | flops 1966080 | bytes 787088 | tf_op jit(solution)/shard_map/while/body/eval_jaxpr/pbq,bq->pb/dot_general | solution.py:69
  154.1 2.9 %fusion.184 = f32[32,32,4,32]{3,1,2,0:T(8,128)S(1)} fusion(f32[32,32,32]{2,1,0:T(8,128)S(1)} %get-tuple-element.723, f32[4,32]{0,1:T(8,128)S(1)} %copy.83, f32[32,32,32]{2,1,0:T(8,128)S(1)} %get-tuple-element.731, f32[32]{0:T(128)S(1)} %bitcast.320, f32[4]{0:T(128)S(1)} %get-tuple-element.732, f32[32,32,32]{2,1,0:T(8,128)S(1)} %get-tuple-element.733, ...), kind=kOutput, calls=%fused_computation.100.clone.1 | convolution fusion | flops 51576832 | bytes 955408 | tf_op jit(solution)/shard_map/while/body/eval_jaxpr/vmap(jvp(bij,bjk->bik))/dot_general | solution.py:53
  157.7 2.2 %bitcast_select_fusion.2 = f32[4,32,32,32]{3,2,0,1:T(8,128)S(1)} fusion(f32[32,32,4,32]{3,1,2,0:T(8,128)S(1)} %fusion.184, f32[4,32,32]{2,0,1:T(4,128)S(1)} %get-tuple-element.743, f32[32,32]{1,0:T(8,128)S(1)} %get-tuple-element.744, f32[32,32]{1,0:T(8,128)S(1)} %get-tuple-element.745, f32[4,32,32]{2,0,1:T(4,128)S(1)} %get-tuple-element.746, ...), kind=kOutput, calls=%fused_computation.99.clone.1 | convolution fusion | flops 50921472 | bytes 1093920 | tf_op jit(solution)/shard_map/while/body/eval_jaxpr/vmap(jvp(bik,blk->bil))/dot_general | solution.py:54
  161.0 1.0 fusion.185
  162.0 1.1 convolution_select_fusion.5
  163.3 2.3 %fusion.187 = f32[4,4,4,32]{1,2,3,0:T(4,128)S(1)} fusion(f32[4,4,4,32]{1,2,3,0:T(4,128)S(1)} %get-tuple-element.787, s32[]{:T(128)} %get-tuple-element.785, f32[4,32,1024]{2,0,1:T(4,128)S(1)} %reshape.2358, f32[32]{0:T(128)S(1)} %get-tuple-element.747, f32[32,1024]{1,0:T(8,128)S(1)} %mul.2955, f32[4]{0:T(128)S(1)} %get-tuple-element.748, ...), kind=kOutput, calls=%fused_computation.113.clone.1 | convolution fusion | flops 6685184 | bytes 722436 | tf_op jit(solution)/shard_map/while/body/eval_jaxpr/pbq,rbq->prb/dot_general | solution.py:71
  165.6 2.2 %fusion.186 = f32[32,1,4]{2,1,0:T(1,128)S(1)} fusion(f32[4,32,1024]{2,0,1:T(4,128)S(1)} %reshape.2358, f32[32]{0:T(128)S(1)} %get-tuple-element.747, f32[32,1024]{1,0:T(8,128)S(1)} %mul.2955, f32[4]{0:T(128)S(1)} %get-tuple-element.748, f32[32,1024,1]{1,0,2:T(8,128)S(1)} %dynamic-slice_bitcast_fusion.2), kind=kOutput, calls=%fused_computation.131.clone.1 | convolution fusion | flops 1966080 | bytes 787088 | tf_op jit(solution)/shard_map/while/body/eval_jaxpr/pbq,bq->pb/dot_general | solution.py:69
  170.3 2.9 %fusion.184 = f32[32,32,4,32]{3,1,2,0:T(8,128)S(1)} fusion(f32[32,32,32]{2,1,0:T(8,128)S(1)} %get-tuple-element.723, f32[4,32]{0,1:T(8,128)S(1)} %copy.83, f32[32,32,32]{2,1,0:T(8,128)S(1)} %get-tuple-element.731, f32[32]{0:T(128)S(1)} %bitcast.320, f32[4]{0:T(128)S(1)} %get-tuple-element.732, f32[32,32,32]{2,1,0:T(8,128)S(1)} %get-tuple-element.733, ...), kind=kOutput, calls=%fused_computation.100.clone.1 | convolution fusion | flops 51576832 | bytes 955408 | tf_op jit(solution)/shard_map/while/body/eval_jaxpr/vmap(jvp(bij,bjk->bik))/dot_general | solution.py:53
  173.9 2.2 %bitcast_select_fusion.2 = f32[4,32,32,32]{3,2,0,1:T(8,128)S(1)} fusion(f32[32,32,4,32]{3,1,2,0:T(8,128)S(1)} %fusion.184, f32[4,32,32]{2,0,1:T(4,128)S(1)} %get-tuple-element.743, f32[32,32]{1,0:T(8,128)S(1)} %get-tuple-element.744, f32[32,32]{1,0:T(8,128)S(1)} %get-tuple-element.745, f32[4,32,32]{2,0,1:T(4,128)S(1)} %get-tuple-element.746, ...), kind=kOutput, calls=%fused_computation.99.clone.1 | convolution fusion | flops 50921472 | bytes 1093920 | tf_op jit(solution)/shard_map/while/body/eval_jaxpr/vmap(jvp(bik,blk->bil))/dot_general | solution.py:54
  177.1 1.0 fusion.185
  178.1 1.1 convolution_select_fusion.5
  179.4 2.3 %fusion.187 = f32[4,4,4,32]{1,2,3,0:T(4,128)S(1)} fusion(f32[4,4,4,32]{1,2,3,0:T(4,128)S(1)} %get-tuple-element.787, s32[]{:T(128)} %get-tuple-element.785, f32[4,32,1024]{2,0,1:T(4,128)S(1)} %reshape.2358, f32[32]{0:T(128)S(1)} %get-tuple-element.747, f32[32,1024]{1,0:T(8,128)S(1)} %mul.2955, f32[4]{0:T(128)S(1)} %get-tuple-element.748, ...), kind=kOutput, calls=%fused_computation.113.clone.1 | convolution fusion | flops 6685184 | bytes 722436 | tf_op jit(solution)/shard_map/while/body/eval_jaxpr/pbq,rbq->prb/dot_general | solution.py:71
  181.8 2.2 %fusion.186 = f32[32,1,4]{2,1,0:T(1,128)S(1)} fusion(f32[4,32,1024]{2,0,1:T(4,128)S(1)} %reshape.2358, f32[32]{0:T(128)S(1)} %get-tuple-element.747, f32[32,1024]{1,0:T(8,128)S(1)} %mul.2955, f32[4]{0:T(128)S(1)} %get-tuple-element.748, f32[32,1024,1]{1,0,2:T(8,128)S(1)} %dynamic-slice_bitcast_fusion.2), kind=kOutput, calls=%fused_computation.131.clone.1 | convolution fusion | flops 1966080 | bytes 787088 | tf_op jit(solution)/shard_map/while/body/eval_jaxpr/pbq,bq->pb/dot_general | solution.py:69
  186.5 2.9 %fusion.184 = f32[32,32,4,32]{3,1,2,0:T(8,128)S(1)} fusion(f32[32,32,32]{2,1,0:T(8,128)S(1)} %get-tuple-element.723, f32[4,32]{0,1:T(8,128)S(1)} %copy.83, f32[32,32,32]{2,1,0:T(8,128)S(1)} %get-tuple-element.731, f32[32]{0:T(128)S(1)} %bitcast.320, f32[4]{0:T(128)S(1)} %get-tuple-element.732, f32[32,32,32]{2,1,0:T(8,128)S(1)} %get-tuple-element.733, ...), kind=kOutput, calls=%fused_computation.100.clone.1 | convolution fusion | flops 51576832 | bytes 955408 | tf_op jit(solution)/shard_map/while/body/eval_jaxpr/vmap(jvp(bij,bjk->bik))/dot_general | solution.py:53
  190.1 2.2 %bitcast_select_fusion.2 = f32[4,32,32,32]{3,2,0,1:T(8,128)S(1)} fusion(f32[32,32,4,32]{3,1,2,0:T(8,128)S(1)} %fusion.184, f32[4,32,32]{2,0,1:T(4,128)S(1)} %get-tuple-element.743, f32[32,32]{1,0:T(8,128)S(1)} %get-tuple-element.744, f32[32,32]{1,0:T(8,128)S(1)} %get-tuple-element.745, f32[4,32,32]{2,0,1:T(4,128)S(1)} %get-tuple-element.746, ...), kind=kOutput, calls=%fused_computation.99.clone.1 | convolution fusion | flops 50921472 | bytes 1093920 | tf_op jit(solution)/shard_map/while/body/eval_jaxpr/vmap(jvp(bik,blk->bil))/dot_general | solution.py:54
  194.4 1.1 convolution_select_fusion.5
  195.7 2.3 %fusion.187 = f32[4,4,4,32]{1,2,3,0:T(4,128)S(1)} fusion(f32[4,4,4,32]{1,2,3,0:T(4,128)S(1)} %get-tuple-element.787, s32[]{:T(128)} %get-tuple-element.785, f32[4,32,1024]{2,0,1:T(4,128)S(1)} %reshape.2358, f32[32]{0:T(128)S(1)} %get-tuple-element.747, f32[32,1024]{1,0:T(8,128)S(1)} %mul.2955, f32[4]{0:T(128)S(1)} %get-tuple-element.748, ...), kind=kOutput, calls=%fused_computation.113.clone.1 | convolution fusion | flops 6685184 | bytes 722436 | tf_op jit(solution)/shard_map/while/body/eval_jaxpr/pbq,rbq->prb/dot_general | solution.py:71
  198.0 2.2 %fusion.186 = f32[32,1,4]{2,1,0:T(1,128)S(1)} fusion(f32[4,32,1024]{2,0,1:T(4,128)S(1)} %reshape.2358, f32[32]{0:T(128)S(1)} %get-tuple-element.747, f32[32,1024]{1,0:T(8,128)S(1)} %mul.2955, f32[4]{0:T(128)S(1)} %get-tuple-element.748, f32[32,1024,1]{1,0,2:T(8,128)S(1)} %dynamic-slice_bitcast_fusion.2), kind=kOutput, calls=%fused_computation.131.clone.1 | convolution fusion | flops 1966080 | bytes 787088 | tf_op jit(solution)/shard_map/while/body/eval_jaxpr/pbq,bq->pb/dot_general | solution.py:69
  200.9 1.3 fusion.143
  (243 shorter events, 39.1 us)
Async XLA Ops:
  4.2 37.6 %all-to-all-start = ((s32[64,4,1]{1,2,0:T(1,128)}), s32[64,4,1]{1,2,0:T(1,128)S(1)}, u32[]{:S(2)}, u32[]{:S(2)}) async-start(s32[64,4,1]{1,2,0:T(1,128)} %bitcast.49), calls=%async_computation | async-start | bytes 65536 | tf_op jit(solution)/shard_map/all_to_all | solution.py:172
  40.5 14.2 %copy-start.2 = (f32[32]{0:T(128)S(1)}, f32[32]{0:T(128)}, u32[]{:S(2)}) copy-start(f32[32]{0:T(128)} %param.19) | copy-start | bytes 388
  41.8 48.8 %copy-start = (f32[32,1024]{1,0:T(8,128)S(1)}, f32[32,1024]{1,0:T(8,128)}, u32[]{:S(2)}) copy-start(f32[32,1024]{1,0:T(8,128)} %param.18) | copy-start | bytes 393220
  41.8 42.0 %all-to-all-start.1 = ((f32[64,4,1024]{2,1,0:T(4,128)}), f32[64,4,1024]{2,1,0:T(4,128)S(1)}, u32[]{:S(2)}, u32[]{:S(2)}) async-start(f32[64,4,1024]{2,1,0:T(4,128)} %all_to_all.32), calls=%async_computation.1 | async-start | bytes 2097152 | tf_op jit(solution)/shard_map/all_to_all | solution.py:171
  83.8 18.5 %all-to-all-start.3 = ((f32[64,4,1]{1,2,0:T(1,128)}), f32[64,4,1]{1,2,0:T(1,128)S(1)}, u32[]{:S(2)}, u32[]{:S(2)}) async-start(f32[64,4,1]{1,2,0:T(1,128)} %bitcast.55), calls=%async_computation.3 | async-start | bytes 65536 | tf_op jit(solution)/shard_map/all_to_all | solution.py:177
  102.3 32.5 %all-to-all-start.2 = ((f32[64,4,1024]{2,1,0:T(4,128)}), f32[64,4,1024]{2,1,0:T(4,128)S(1)}, u32[]{:S(2)}, u32[]{:S(2)}) async-start(f32[64,4,1024]{2,1,0:T(4,128)} %all_to_all.35), calls=%async_computation.2 | async-start | bytes 2097152 | tf_op jit(solution)/shard_map/all_to_all | solution.py:176
  135.9 68.4 %copy-start.1 = (f32[4,128]{1,0:T(4,128)S(1)}, f32[4,128]{1,0:T(4,128)}, u32[]{:S(2)}) copy-start(f32[4,128]{1,0:T(4,128)} %param.12) | copy-start | bytes 6148
where the time goes:
time: 206 us; the launch traced here: 205 us
  matrix products  57.5 us (28%)
  waiting for transfers between devices  48.6 us (24%)
  starting transfers between devices  40.5 us (20%)
  local copies, waits for them, and re-layouts  26.4 us (13%)
  other arithmetic  18.7 us (9%)
  blocking collectives  11.2 us (5%)
    all_to_all x1, waiting for transfers between devices, shards(): lax.all_to_all(outgoing, 'brick', split_axis=0, concat_axis=0, tiled=True)  26.7 us
    dot_general x12, matrix products, render(): blurred = jnp.einsum('bij,bjk->bik', kernel, galaxy, precision=highest)  19.7 us
    dot_general x12, matrix products, render(): blurred = jnp.einsum('bik,blk->bil', blurred, kernel, precision=highest)  17.4 us
    all_to_all x1, starting transfers between devices, shards(): lax.all_to_all(outgoing_cells, 'brick', split_axis=0, concat_axis=0, tile...  16.6 us
    all_to_all x1, waiting for transfers between devices, shards(): lax.all_to_all(slot_rows, 'brick', split_axis=0, concat_axis=0, tiled=True)  13.4 us
    all_to_all x1, starting transfers between devices, shards(): lax.all_to_all(outgoing, 'brick', split_axis=0, concat_axis=0, tiled=True)  12.8 us
    psum x1, blocking collectives, shards(): group_chi = lax.psum(local_chi, 'blk')  11.2 us
    dot_general x4, matrix products, source_moments(): jnp.einsum('pbq,rbq->prb', jacobian, jacobian, precision=highest)  9.38 us
  transfers between devices with their start and end apart: 4, of which 3 were waited for; matrix products, arithmetic and copies ran while one was open for 12% of the time, Pallas kernels for 0%

commit v1 on v0

--- a/solution.py
+++ b/solution.py
@@ -179,7 +179,11 @@
     gradient, curvature = blocked_moments(
         parameters, sersic, psf_width, point_flag, returned[slot_of], returned_weights[slot_of]
     )
-    group_chi = lax.psum(local_chi, "blk")
+    size = lax.axis_size("blk")
+    group_chi, far = (local_chi, 1)
+    while far < size:
+        group_chi = group_chi + lax.ppermute(group_chi, "blk", [(i, i ^ far) for i in range(size)])
+        far = 2 * far
     damping = base_damping + misfit_scale * group_chi / pixel_total
     return parameters + damped_solve(curvature, gradient, damping)
 

time: 206 us -> 206 us (level)
  blocking collectives: 11.2 us -> 0 us
  starting transfers between devices: 40.5 us -> 51 us
    psum x1 -> x0, blocking collectives: 11.2 us -> none  [shards(): group_chi = lax.psum(local_chi, 'blk')]
    ppermute x0 -> x3, starting transfers between devices: none -> 10.5 us  [shards(): lax.ppermute(group_chi, 'blk', [(i, i ^ far) for i in range(size)])]
    all_to_all x1, waiting for transfers between devices: 13.4 us -> 7.09 us  [shards(): lax.all_to_all(slot_rows, 'brick', split_axis=0, concat_axis=0, tiled=True)]
    ppermute x0 -> x3, waiting for transfers between devices: none -> 5.04 us  [shards(): lax.ppermute(group_chi, 'blk', [(i, i ^ far) for i in range(size)])]
  transfers between devices with their start and end apart: 4 -> 7, of which waited for: 3 -> 6; matrix products, arithmetic and copies ran while one was open for 12% -> 12% of each run, Pallas kernels for 0% -> 0%
where the time goes in v1:
time: 206 us; the launch traced here: 205 us
  matrix products  57.5 us (28%)
  starting transfers between devices  51 us (25%)
  waiting for transfers between devices  47.4 us (23%)
  local copies, waits for them, and re-layouts  26.4 us (13%)
  other arithmetic  18.7 us (9%)
  between operations  2.73 us (1%)
    all_to_all x1, waiting for transfers between devices, shards(): lax.all_to_all(outgoing, 'brick', split_axis=0, concat_axis=0, tiled=True)  26.7 us
    dot_general x12, matrix products, render(): blurred = jnp.einsum('bij,bjk->bik', kernel, galaxy, precision=highest)  19.7 us
    dot_general x12, matrix products, render(): blurred = jnp.einsum('bik,blk->bil', blurred, kernel, precision=highest)  17.4 us
    all_to_all x1, starting transfers between devices, shards(): lax.all_to_all(outgoing_cells, 'brick', split_axis=0, concat_axis=0, tile...  16.6 us
    all_to_all x1, starting transfers between devices, shards(): lax.all_to_all(outgoing, 'brick', split_axis=0, concat_axis=0, tiled=True)  12.8 us
    ppermute x3, starting transfers between devices, shards(): lax.ppermute(group_chi, 'blk', [(i, i ^ far) for i in range(size)])  10.5 us
    dot_general x4, matrix products, source_moments(): jnp.einsum('pbq,rbq->prb', jacobian, jacobian, precision=highest)  9.38 us
    dot_general x4, matrix products, source_moments(): jnp.einsum('pbq,bq->pb', jacobian, weighted_rows, precision=highest)  8.96 us
  transfers between devices with their start and end apart: 7, of which 6 were waited for; matrix products, arithmetic and copies ran while one was open for 12% of the time, Pallas kernels for 0%

profile of v1, /device:TPU:6, one launch (start us, length us, event | category | flops | bytes accessed | tf_op | source)
XLA Modules:
  0.0 205.0 jit_solution(6794515072890308651)
XLA Ops:
  2.4 1.1 scatter_custom_fusion
  4.2 16.6 %all-to-all-start = ((s32[64,4,1]{1,2,0:T(1,128)}), s32[64,4,1]{1,2,0:T(1,128)S(1)}, u32[]{:S(2)}, u32[]{:S(2)}) async-start(s32[64,4,1]{1,2,0:T(1,128)} %bitcast.49), calls=%async_computation | async-start | bytes 65536 | tf_op jit(solution)/shard_map/all_to_all | solution.py:172
  21.6 1.3 reshape.2269
  24.4 14.8 %while.32 = (s32[]{:T(128)}, f32[4,32,1024]{2,1,0:T(8,128)S(1)}, f32[4,4,32]{2,1,0:T(4,128)S(1)}, s32[4,32]{1,0:T(4,128)}, f32[4,32]{1,0:T(4,128)S(1)}, /*index=5*/f32[4,32]{1,0:T(4,128)S(1)}, s32[]{:T(128)}, f32[]{:T(128)}) while((s32[]{:T(128)}, f32[4,32,1024]{2,1,0:T(8,128)S(1)}, f32[4,4,32]{2,1,0:T(4,128)S(1)}, s32[4,32]{1,0:T(4,128)}, ...), condition=%wide.region_6.7_spmd, body=%wide.region_3.6_spmd.sunk | while | flops 25907552 | bytes 1019813 | solution.py:117
  25.0 1.0 fusion.172
  26.7 1.0 convolution_select_fusion.4
  30.4 1.0 convolution_select_fusion.4
  34.1 1.0 convolution_select_fusion.4
  37.8 1.0 convolution_select_fusion.4
  39.2 1.3 scatter_custom_fusion.1
  40.5 1.3 all_to_all.32
  41.8 12.8 %all-to-all-start.1 = ((f32[64,4,1024]{2,1,0:T(4,128)}), f32[64,4,1024]{2,1,0:T(4,128)S(1)}, u32[]{:S(2)}, u32[]{:S(2)}) async-start(f32[64,4,1024]{2,1,0:T(4,128)} %all_to_all.32), calls=%async_computation.1 | async-start | bytes 2097152 | tf_op jit(solution)/shard_map/all_to_all | solution.py:171
  57.1 26.7 %all-to-all-done.1 = f32[64,4,1024]{2,1,0:T(4,128)S(1)} async-done(((f32[64,4,1024]{2,1,0:T(4,128)}), f32[64,4,1024]{2,1,0:T(4,128)S(1)}, u32[]{:S(2)}, u32[]{:S(2)}) %all-to-all-start.1) | async-done | bytes 1048608 | tf_op jit(solution)/shard_map/all_to_all | solution.py:171
  83.8 6.5 %all-to-all-start.3 = ((f32[64,4,1]{1,2,0:T(1,128)}), f32[64,4,1]{1,2,0:T(1,128)S(1)}, u32[]{:S(2)}, u32[]{:S(2)}) async-start(f32[64,4,1]{1,2,0:T(1,128)} %bitcast.55), calls=%async_computation.3 | async-start | bytes 65536 | tf_op jit(solution)/shard_map/all_to_all | solution.py:177
  90.7 1.2 fusion.107
  92.5 1.3 all_to_all.35
  93.8 8.6 %all-to-all-done.3 = f32[64,4,1]{1,2,0:T(1,128)S(1)} async-done(((f32[64,4,1]{1,2,0:T(1,128)}), f32[64,4,1]{1,2,0:T(1,128)S(1)}, u32[]{:S(2)}, u32[]{:S(2)}) %all-to-all-start.3) | async-done | bytes 1056 | tf_op jit(solution)/shard_map/all_to_all | solution.py:177
  102.3 4.7 %all-to-all-start.2 = ((f32[64,4,1024]{2,1,0:T(4,128)}), f32[64,4,1024]{2,1,0:T(4,128)S(1)}, u32[]{:S(2)}, u32[]{:S(2)}) async-start(f32[64,4,1024]{2,1,0:T(4,128)} %all_to_all.35), calls=%async_computation.2 | async-start | bytes 2097152 | tf_op jit(solution)/shard_map/all_to_all | solution.py:176
  108.3 1.3 gather_fusion.1
  109.6 1.9 collective-permute-start
  111.5 1.3 collective-permute-done
  114.1 4.0 %collective-permute-start.1 = (f32[]{:T(128)}, f32[]{:T(128)}, u32[]{:S(2)}, u32[]{:S(2)}) collective-permute-start(f32[]{:T(128)} %add.943), channel_id=1, source_target_pairs={{0,2},{1,3},{2,0},{3,1},{4,6},{5,7},{6,4},{7,5},{8,10},{9,11},{10,... | collective-permute-start | bytes 20 | tf_op jit(solution)/shard_map/ppermute | solution.py:185
  118.1 1.4 collective-permute-done.1
  120.1 4.6 %collective-permute-start.2 = (f32[]{:T(128)}, f32[]{:T(128)}, u32[]{:S(2)}, u32[]{:S(2)}) collective-permute-start(f32[]{:T(128)} %add.944), channel_id=1, source_target_pairs={{0,4},{1,5},{2,6},{3,7},{4,0},{5,1},{6,2},{7,3},{8,12},{9,13},{10,... | collective-permute-start | bytes 20 | tf_op jit(solution)/shard_map/ppermute | solution.py:185
  124.7 2.3 %collective-permute-done.2 = f32[]{:T(128)} collective-permute-done((f32[]{:T(128)}, f32[]{:T(128)}, u32[]{:S(2)}, u32[]{:S(2)}) %collective-permute-start.2) | collective-permute-done | bytes 36 | tf_op jit(solution)/shard_map/ppermute | solution.py:185
  127.7 7.1 %all-to-all-done.2 = f32[64,4,1024]{2,1,0:T(4,128)S(1)} async-done(((f32[64,4,1024]{2,1,0:T(4,128)}), f32[64,4,1024]{2,1,0:T(4,128)S(1)}, u32[]{:S(2)}, u32[]{:S(2)}) %all-to-all-start.2) | async-done | bytes 1048608 | tf_op jit(solution)/shard_map/all_to_all | solution.py:176
  135.9 65.0 %while.33 = (s32[]{:T(128)}, f32[4,4,32]{2,1,0:T(4,128)}, f32[4,4,4,32]{1,2,3,0:T(4,128)S(1)}, f32[4,32,1024]{2,1,0:T(8,128)S(1)}, s32[4,32]{1,0:T(4,128)}, /*in...) while((s32[]{:T(128)}, f32[4,4,32]{2,1,0:T(4,128)}, ...), condition=%wide.region_13.14_spmd, body=%wide.region_8.13_spmd.sunk | while | flops 138444880 | bytes 6357045 | solution.py:132
  137.9 2.9 %fusion.184 = f32[32,32,4,32]{3,1,2,0:T(8,128)S(1)} fusion(f32[32,32,32]{2,1,0:T(8,128)S(1)} %get-tuple-element.723, f32[4,32]{0,1:T(8,128)S(1)} %copy.83, f32[32,32,32]{2,1,0:T(8,128)S(1)} %get-tuple-element.731, f32[32]{0:T(128)S(1)} %bitcast.320, f32[4]{0:T(128)S(1)} %get-tuple-element.732, f32[32,32,32]{2,1,0:T(8,128)S(1)} %get-tuple-element.733, ...), kind=kOutput, calls=%fused_computation.100.clone.1 | convolution fusion | flops 51576832 | bytes 955408 | tf_op jit(solution)/shard_map/while/body/eval_jaxpr/vmap(jvp(bij,bjk->bik))/dot_general | solution.py:53
  141.5 2.2 %bitcast_select_fusion.2 = f32[4,32,32,32]{3,2,0,1:T(8,128)S(1)} fusion(f32[32,32,4,32]{3,1,2,0:T(8,128)S(1)} %fusion.184, f32[4,32,32]{2,0,1:T(4,128)S(1)} %get-tuple-element.743, f32[32,32]{1,0:T(8,128)S(1)} %get-tuple-element.744, f32[32,32]{1,0:T(8,128)S(1)} %get-tuple-element.745, f32[4,32,32]{2,0,1:T(4,128)S(1)} %get-tuple-element.746, ...), kind=kOutput, calls=%fused_computation.99.clone.1 | convolution fusion | flops 50921472 | bytes 1093920 | tf_op jit(solution)/shard_map/while/body/eval_jaxpr/vmap(jvp(bik,blk->bil))/dot_general | solution.py:54
  145.8 1.1 convolution_select_fusion.5
  147.1 2.3 %fusion.187 = f32[4,4,4,32]{1,2,3,0:T(4,128)S(1)} fusion(f32[4,4,4,32]{1,2,3,0:T(4,128)S(1)} %get-tuple-element.787, s32[]{:T(128)} %get-tuple-element.785, f32[4,32,1024]{2,0,1:T(4,128)S(1)} %reshape.2358, f32[32]{0:T(128)S(1)} %get-tuple-element.747, f32[32,1024]{1,0:T(8,128)S(1)} %mul.2955, f32[4]{0:T(128)S(1)} %get-tuple-element.748, ...), kind=kOutput, calls=%fused_computation.113.clone.1 | convolution fusion | flops 6685184 | bytes 722436 | tf_op jit(solution)/shard_map/while/body/eval_jaxpr/pbq,rbq->prb/dot_general | solution.py:71
  149.4 2.2 %fusion.186 = f32[32,1,4]{2,1,0:T(1,128)S(1)} fusion(f32[4,32,1024]{2,0,1:T(4,128)S(1)} %reshape.2358, f32[32]{0:T(128)S(1)} %get-tuple-element.747, f32[32,1024]{1,0:T(8,128)S(1)} %mul.2955, f32[4]{0:T(128)S(1)} %get-tuple-element.748, f32[32,1024,1]{1,0,2:T(8,128)S(1)} %dynamic-slice_bitcast_fusion.2), kind=kOutput, calls=%fused_computation.131.clone.1 | convolution fusion | flops 1966080 | bytes 787088 | tf_op jit(solution)/shard_map/while/body/eval_jaxpr/pbq,bq->pb/dot_general | solution.py:69
  154.1 2.9 %fusion.184 = f32[32,32,4,32]{3,1,2,0:T(8,128)S(1)} fusion(f32[32,32,32]{2,1,0:T(8,128)S(1)} %get-tuple-element.723, f32[4,32]{0,1:T(8,128)S(1)} %copy.83, f32[32,32,32]{2,1,0:T(8,128)S(1)} %get-tuple-element.731, f32[32]{0:T(128)S(1)} %bitcast.320, f32[4]{0:T(128)S(1)} %get-tuple-element.732, f32[32,32,32]{2,1,0:T(8,128)S(1)} %get-tuple-element.733, ...), kind=kOutput, calls=%fused_computation.100.clone.1 | convolution fusion | flops 51576832 | bytes 955408 | tf_op jit(solution)/shard_map/while/body/eval_jaxpr/vmap(jvp(bij,bjk->bik))/dot_general | solution.py:53
  157.7 2.2 %bitcast_select_fusion.2 = f32[4,32,32,32]{3,2,0,1:T(8,128)S(1)} fusion(f32[32,32,4,32]{3,1,2,0:T(8,128)S(1)} %fusion.184, f32[4,32,32]{2,0,1:T(4,128)S(1)} %get-tuple-element.743, f32[32,32]{1,0:T(8,128)S(1)} %get-tuple-element.744, f32[32,32]{1,0:T(8,128)S(1)} %get-tuple-element.745, f32[4,32,32]{2,0,1:T(4,128)S(1)} %get-tuple-element.746, ...), kind=kOutput, calls=%fused_computation.99.clone.1 | convolution fusion | flops 50921472 | bytes 1093920 | tf_op jit(solution)/shard_map/while/body/eval_jaxpr/vmap(jvp(bik,blk->bil))/dot_general | solution.py:54
  162.0 1.1 convolution_select_fusion.5
  163.3 2.3 %fusion.187 = f32[4,4,4,32]{1,2,3,0:T(4,128)S(1)} fusion(f32[4,4,4,32]{1,2,3,0:T(4,128)S(1)} %get-tuple-element.787, s32[]{:T(128)} %get-tuple-element.785, f32[4,32,1024]{2,0,1:T(4,128)S(1)} %reshape.2358, f32[32]{0:T(128)S(1)} %get-tuple-element.747, f32[32,1024]{1,0:T(8,128)S(1)} %mul.2955, f32[4]{0:T(128)S(1)} %get-tuple-element.748, ...), kind=kOutput, calls=%fused_computation.113.clone.1 | convolution fusion | flops 6685184 | bytes 722436 | tf_op jit(solution)/shard_map/while/body/eval_jaxpr/pbq,rbq->prb/dot_general | solution.py:71
  165.6 2.2 %fusion.186 = f32[32,1,4]{2,1,0:T(1,128)S(1)} fusion(f32[4,32,1024]{2,0,1:T(4,128)S(1)} %reshape.2358, f32[32]{0:T(128)S(1)} %get-tuple-element.747, f32[32,1024]{1,0:T(8,128)S(1)} %mul.2955, f32[4]{0:T(128)S(1)} %get-tuple-element.748, f32[32,1024,1]{1,0,2:T(8,128)S(1)} %dynamic-slice_bitcast_fusion.2), kind=kOutput, calls=%fused_computation.131.clone.1 | convolution fusion | flops 1966080 | bytes 787088 | tf_op jit(solution)/shard_map/while/body/eval_jaxpr/pbq,bq->pb/dot_general | solution.py:69
  170.3 2.9 %fusion.184 = f32[32,32,4,32]{3,1,2,0:T(8,128)S(1)} fusion(f32[32,32,32]{2,1,0:T(8,128)S(1)} %get-tuple-element.723, f32[4,32]{0,1:T(8,128)S(1)} %copy.83, f32[32,32,32]{2,1,0:T(8,128)S(1)} %get-tuple-element.731, f32[32]{0:T(128)S(1)} %bitcast.320, f32[4]{0:T(128)S(1)} %get-tuple-element.732, f32[32,32,32]{2,1,0:T(8,128)S(1)} %get-tuple-element.733, ...), kind=kOutput, calls=%fused_computation.100.clone.1 | convolution fusion | flops 51576832 | bytes 955408 | tf_op jit(solution)/shard_map/while/body/eval_jaxpr/vmap(jvp(bij,bjk->bik))/dot_general | solution.py:53
  173.9 2.2 %bitcast_select_fusion.2 = f32[4,32,32,32]{3,2,0,1:T(8,128)S(1)} fusion(f32[32,32,4,32]{3,1,2,0:T(8,128)S(1)} %fusion.184, f32[4,32,32]{2,0,1:T(4,128)S(1)} %get-tuple-element.743, f32[32,32]{1,0:T(8,128)S(1)} %get-tuple-element.744, f32[32,32]{1,0:T(8,128)S(1)} %get-tuple-element.745, f32[4,32,32]{2,0,1:T(4,128)S(1)} %get-tuple-element.746, ...), kind=kOutput, calls=%fused_computation.99.clone.1 | convolution fusion | flops 50921472 | bytes 1093920 | tf_op jit(solution)/shard_map/while/body/eval_jaxpr/vmap(jvp(bik,blk->bil))/dot_general | solution.py:54
  178.1 1.1 convolution_select_fusion.5
  179.4 2.3 %fusion.187 = f32[4,4,4,32]{1,2,3,0:T(4,128)S(1)} fusion(f32[4,4,4,32]{1,2,3,0:T(4,128)S(1)} %get-tuple-element.787, s32[]{:T(128)} %get-tuple-element.785, f32[4,32,1024]{2,0,1:T(4,128)S(1)} %reshape.2358, f32[32]{0:T(128)S(1)} %get-tuple-element.747, f32[32,1024]{1,0:T(8,128)S(1)} %mul.2955, f32[4]{0:T(128)S(1)} %get-tuple-element.748, ...), kind=kOutput, calls=%fused_computation.113.clone.1 | convolution fusion | flops 6685184 | bytes 722436 | tf_op jit(solution)/shard_map/while/body/eval_jaxpr/pbq,rbq->prb/dot_general | solution.py:71
  181.8 2.2 %fusion.186 = f32[32,1,4]{2,1,0:T(1,128)S(1)} fusion(f32[4,32,1024]{2,0,1:T(4,128)S(1)} %reshape.2358, f32[32]{0:T(128)S(1)} %get-tuple-element.747, f32[32,1024]{1,0:T(8,128)S(1)} %mul.2955, f32[4]{0:T(128)S(1)} %get-tuple-element.748, f32[32,1024,1]{1,0,2:T(8,128)S(1)} %dynamic-slice_bitcast_fusion.2), kind=kOutput, calls=%fused_computation.131.clone.1 | convolution fusion | flops 1966080 | bytes 787088 | tf_op jit(solution)/shard_map/while/body/eval_jaxpr/pbq,bq->pb/dot_general | solution.py:69
  186.5 2.9 %fusion.184 = f32[32,32,4,32]{3,1,2,0:T(8,128)S(1)} fusion(f32[32,32,32]{2,1,0:T(8,128)S(1)} %get-tuple-element.723, f32[4,32]{0,1:T(8,128)S(1)} %copy.83, f32[32,32,32]{2,1,0:T(8,128)S(1)} %get-tuple-element.731, f32[32]{0:T(128)S(1)} %bitcast.320, f32[4]{0:T(128)S(1)} %get-tuple-element.732, f32[32,32,32]{2,1,0:T(8,128)S(1)} %get-tuple-element.733, ...), kind=kOutput, calls=%fused_computation.100.clone.1 | convolution fusion | flops 51576832 | bytes 955408 | tf_op jit(solution)/shard_map/while/body/eval_jaxpr/vmap(jvp(bij,bjk->bik))/dot_general | solution.py:53
  190.1 2.2 %bitcast_select_fusion.2 = f32[4,32,32,32]{3,2,0,1:T(8,128)S(1)} fusion(f32[32,32,4,32]{3,1,2,0:T(8,128)S(1)} %fusion.184, f32[4,32,32]{2,0,1:T(4,128)S(1)} %get-tuple-element.743, f32[32,32]{1,0:T(8,128)S(1)} %get-tuple-element.744, f32[32,32]{1,0:T(8,128)S(1)} %get-tuple-element.745, f32[4,32,32]{2,0,1:T(4,128)S(1)} %get-tuple-element.746, ...), kind=kOutput, calls=%fused_computation.99.clone.1 | convolution fusion | flops 50921472 | bytes 1093920 | tf_op jit(solution)/shard_map/while/body/eval_jaxpr/vmap(jvp(bik,blk->bil))/dot_general | solution.py:54
  194.4 1.1 convolution_select_fusion.5
  195.7 2.3 %fusion.187 = f32[4,4,4,32]{1,2,3,0:T(4,128)S(1)} fusion(f32[4,4,4,32]{1,2,3,0:T(4,128)S(1)} %get-tuple-element.787, s32[]{:T(128)} %get-tuple-element.785, f32[4,32,1024]{2,0,1:T(4,128)S(1)} %reshape.2358, f32[32]{0:T(128)S(1)} %get-tuple-element.747, f32[32,1024]{1,0:T(8,128)S(1)} %mul.2955, f32[4]{0:T(128)S(1)} %get-tuple-element.748, ...), kind=kOutput, calls=%fused_computation.113.clone.1 | convolution fusion | flops 6685184 | bytes 722436 | tf_op jit(solution)/shard_map/while/body/eval_jaxpr/pbq,rbq->prb/dot_general | solution.py:71
  198.0 2.2 %fusion.186 = f32[32,1,4]{2,1,0:T(1,128)S(1)} fusion(f32[4,32,1024]{2,0,1:T(4,128)S(1)} %reshape.2358, f32[32]{0:T(128)S(1)} %get-tuple-element.747, f32[32,1024]{1,0:T(8,128)S(1)} %mul.2955, f32[4]{0:T(128)S(1)} %get-tuple-element.748, f32[32,1024,1]{1,0,2:T(8,128)S(1)} %dynamic-slice_bitcast_fusion.2), kind=kOutput, calls=%fused_computation.131.clone.1 | convolution fusion | flops 1966080 | bytes 787088 | tf_op jit(solution)/shard_map/while/body/eval_jaxpr/pbq,bq->pb/dot_general | solution.py:69
  200.9 1.3 fusion.143
  (248 shorter events, 44.1 us)
Async XLA Ops:
  4.2 37.6 %all-to-all-start = ((s32[64,4,1]{1,2,0:T(1,128)}), s32[64,4,1]{1,2,0:T(1,128)S(1)}, u32[]{:S(2)}, u32[]{:S(2)}) async-start(s32[64,4,1]{1,2,0:T(1,128)} %bitcast.49), calls=%async_computation | async-start | bytes 65536 | tf_op jit(solution)/shard_map/all_to_all | solution.py:172
  40.5 14.2 %copy-start.2 = (f32[32]{0:T(128)S(1)}, f32[32]{0:T(128)}, u32[]{:S(2)}) copy-start(f32[32]{0:T(128)} %param.19) | copy-start | bytes 388
  41.8 48.8 %copy-start = (f32[32,1024]{1,0:T(8,128)S(1)}, f32[32,1024]{1,0:T(8,128)}, u32[]{:S(2)}) copy-start(f32[32,1024]{1,0:T(8,128)} %param.18) | copy-start | bytes 393220
  41.8 42.0 %all-to-all-start.1 = ((f32[64,4,1024]{2,1,0:T(4,128)}), f32[64,4,1024]{2,1,0:T(4,128)S(1)}, u32[]{:S(2)}, u32[]{:S(2)}) async-start(f32[64,4,1024]{2,1,0:T(4,128)} %all_to_all.32), calls=%async_computation.1 | async-start | bytes 2097152 | tf_op jit(solution)/shard_map/all_to_all | solution.py:171
  83.8 18.5 %all-to-all-start.3 = ((f32[64,4,1]{1,2,0:T(1,128)}), f32[64,4,1]{1,2,0:T(1,128)S(1)}, u32[]{:S(2)}, u32[]{:S(2)}) async-start(f32[64,4,1]{1,2,0:T(1,128)} %bitcast.55), calls=%async_computation.3 | async-start | bytes 65536 | tf_op jit(solution)/shard_map/all_to_all | solution.py:177
  102.3 32.5 %all-to-all-start.2 = ((f32[64,4,1024]{2,1,0:T(4,128)}), f32[64,4,1024]{2,1,0:T(4,128)S(1)}, u32[]{:S(2)}, u32[]{:S(2)}) async-start(f32[64,4,1024]{2,1,0:T(4,128)} %all_to_all.35), calls=%async_computation.2 | async-start | bytes 2097152 | tf_op jit(solution)/shard_map/all_to_all | solution.py:176
  109.6 3.2 %collective-permute-start = (f32[]{:T(128)}, f32[]{:T(128)}, u32[]{:S(2)}, u32[]{:S(2)}) collective-permute-start(f32[]{:T(128)} %get-tuple-element.534), channel_id=1, source_target_pairs={{0,1},{1,0},{2,3},{3,2},{4,5},{5,4},{6,7},{7,6},{8,9},{9,8},{10,11... | collective-permute-start | bytes 20 | tf_op jit(solution)/shard_map/ppermute | solution.py:185
  114.1 5.4 %collective-permute-start.1 = (f32[]{:T(128)}, f32[]{:T(128)}, u32[]{:S(2)}, u32[]{:S(2)}) collective-permute-start(f32[]{:T(128)} %add.943), channel_id=1, source_target_pairs={{0,2},{1,3},{2,0},{3,1},{4,6},{5,7},{6,4},{7,5},{8,10},{9,11},{10,... | collective-permute-start | bytes 20 | tf_op jit(solution)/shard_map/ppermute | solution.py:185
  120.1 6.9 %collective-permute-start.2 = (f32[]{:T(128)}, f32[]{:T(128)}, u32[]{:S(2)}, u32[]{:S(2)}) collective-permute-start(f32[]{:T(128)} %add.944), channel_id=1, source_target_pairs={{0,4},{1,5},{2,6},{3,7},{4,0},{5,1},{6,2},{7,3},{8,12},{9,13},{10,... | collective-permute-start | bytes 20 | tf_op jit(solution)/shard_map/ppermute | solution.py:185
  135.9 68.4 %copy-start.1 = (f32[4,128]{1,0:T(4,128)S(1)}, f32[4,128]{1,0:T(4,128)}, u32[]{:S(2)}) copy-start(f32[4,128]{1,0:T(4,128)} %param.12) | copy-start | bytes 6148
